TPU v7x, 32 devices: a whole 2x2x4 slice. The times are simulated.
32 devices in a mesh: grp: 2 (over y), tile: 4 (over x, core), tp: 4 (over z).
Axes of the slice: x: 2, y: 2, z: 4, core: 2. Of those that a mesh axis runs over, the one named last changes fastest.
Arguments:
- atmos_state: bfloat16 [4096, 1536], P(('grp', 'tile')), may hold values from -6 to 6
- atmos_gain: float32 [1536], replicated, may hold values from 0.25 to 1.75
- w_first: bfloat16 [1536, 3072], P(('grp', 'tile'), 'tp'), may hold values from -0.15625 to 0.15625
- w_second: bfloat16 [1536, 3072], P(('grp', 'tile'), 'tp'), may hold values from -0.109375 to 0.109375
- flux_proj: bfloat16 [1536, 256], replicated, may hold values from -0.15625 to 0.15625
- remap_index: int32 [64, 3], P(('grp', 'tile', 'tp')), may hold values from 0 to 3
- remap_weight: bfloat16 [64, 3, 128, 128], P(('grp', 'tile', 'tp')), may hold values from -0.3125 to 0.3125
- ocean_state: bfloat16 [64, 128, 256], P(('grp', 'tile'), 'tp'), may hold values from -6 to 6
- depth_levels: int32 [64, 128], P(('grp', 'tile'), 'tp'), may hold values from 0 to 16
- conv_kernel: float32 [3, 3, 256], replicated, may hold values from -2 to 2
- ocean_gain: float32 [256], replicated, may hold values from 0.25 to 1.75
- ocean_w_in: bfloat16 [256, 1024], replicated, may hold values from -0.375 to 0.375
- ocean_w_out: bfloat16 [1024, 256], replicated, may hold values from -0.1875 to 0.1875
- ocean_cotangent: bfloat16 [64, 128, 256], P(('grp', 'tile'), 'tp'), may hold values from -6 to 6
Outputs:
- atmos_out: bfloat16 [4096, 1536], P(('grp', 'tile', 'tp'))
- ocean_out: bfloat16 [64, 128, 256], P(('grp', 'tile'), 'tp')
- weight_grads: float32 [2048, 256], P(('grp', 'tile', 'tp'))
Inputs may be any that keep to these rules, and one draw needn't show every extreme that they name: `remap_index`: index the 128-token blocks among the 512 atmosphere tokens of the same grp and tile indices as the ocean tile of that block. `depth_levels`: 0 marks land.
All inputs are finite; a program needn't handle non-finite values.
Results may differ from a plain program's by a relative error of at most 0.018.
Values may be sent and summed in bfloat16 or wider, within the bound.
No kernel may reach another device: no remote copies, remote signals or barrier semaphores. Data moves between devices by JAX's collectives and lax.ppermute only.
A program may use at most 64 MiB of HBM per device.

v0:
```python
import jax
import jax.numpy as jnp
from jax import lax
from jax.sharding import PartitionSpec as P

LEV = 16
epsilon = 1e-06


def with_halo(block, sides, width):
    for axis, dim in sides:
        count = lax.axis_size(axis)
        forward = [(i, i + 1) for i in range(count - 1)]
        backward = [(target, source) for source, target in forward]
        low = lax.ppermute(
            lax.slice_in_dim(block, block.shape[dim] - width, None, axis=dim), axis, forward
        )
        high = lax.ppermute(lax.slice_in_dim(block, 0, width, axis=dim), axis, backward)
        block = jnp.concatenate([low, block, high], axis=dim)
    return block


def rms_norm(values, gain):
    wide = values.astype(jnp.float32)
    scale = lax.rsqrt(jnp.mean(wide * wide, axis=-1, keepdims=True) + epsilon)
    return (wide * scale * gain).astype(jnp.bfloat16)


def on_device(
    atmos_state,
    atmos_gain,
    w_first,
    w_second,
    flux_proj,
    remap_index,
    remap_weight,
    ocean_state,
    depth_levels,
    conv_kernel,
    ocean_gain,
    ocean_w_in,
    ocean_w_out,
    ocean_cotangent,
):
    normed = rms_norm(atmos_state, atmos_gain)
    rows_all = atmos_state.shape[0]
    hsum = jnp.dot(
        normed,
        lax.all_gather(w_first, ("grp", "tile"), axis=0, tiled=True),
        preferred_element_type=jnp.float32,
    )
    hidden = jax.nn.gelu(hsum).astype(jnp.bfloat16)
    partial_sum = lax.dot_general(
        hidden,
        lax.all_gather(w_second, ("grp", "tile"), axis=0, tiled=True),
        (((1,), (1,)), ((), ())),
        preferred_element_type=jnp.float32,
    )
    rows_own = rows_all // lax.axis_size("tp")
    block_rows = remap_weight.shape[2]
    channels = flux_proj.shape[1]
    summed = lax.psum_scatter(
        partial_sum.astype(jnp.bfloat16), "tp", scatter_dimension=0, tiled=True
    ).astype(jnp.float32)
    own_rows = lax.dynamic_slice_in_dim(atmos_state, lax.axis_index("tp") * rows_own, rows_own, 0)
    atmos_out = (own_rows.astype(jnp.float32) + summed).astype(jnp.bfloat16)
    flux = jnp.dot(atmos_out, flux_proj, preferred_element_type=jnp.float32).astype(jnp.bfloat16)
    piece = lax.all_gather(flux, "tp", axis=0, tiled=True)
    count = piece.shape[0] // block_rows
    blocks = piece.reshape(count, block_rows, channels)
    targets = jnp.arange(count, dtype=jnp.int32)
    select = (remap_index[:, :, None] == targets[None, None, :]).astype(jnp.bfloat16)
    picked = jnp.einsum("bkj,jrc->bkrc", select, blocks, preferred_element_type=jnp.float32).astype(
        jnp.bfloat16
    )
    remapped = jnp.einsum(
        "bksr,bkrc->bsc", remap_weight, picked, preferred_element_type=jnp.float32
    )
    tile_x, tile_y, _ = ocean_state.shape
    levels = jnp.arange(channels, dtype=jnp.int32) // (channels // LEV)
    wet = (levels[None, None, :] < depth_levels[:, :, None]).astype(jnp.float32)
    moved = remapped.astype(jnp.bfloat16).reshape(tile_x, tile_y, channels)
    field = ((ocean_state.astype(jnp.float32) + moved.astype(jnp.float32)) * wet).astype(
        jnp.bfloat16
    )
    padded = with_halo(field, ((("grp", "tile"), 0), ("tp", 1)), 1).astype(jnp.float32)
    conv = jnp.zeros((tile_x, tile_y, channels), jnp.float32)
    for i in range(3):
        for j in range(3):
            conv = conv + conv_kernel[i, j] * padded[i : i + tile_x, j : j + tile_y]
    centred = conv - jnp.mean(conv, axis=-1, keepdims=True)
    variance = jnp.mean(centred * centred, axis=-1, keepdims=True)
    cells = tile_x * tile_y
    ocean_normed = (
        (centred * lax.rsqrt(variance + epsilon) * ocean_gain)
        .astype(jnp.bfloat16)
        .reshape(cells, channels)
    )
    flat_field = field.reshape(cells, channels)
    flat_wet = wet.reshape(cells, channels)
    pre = jnp.dot(ocean_normed, ocean_w_in, preferred_element_type=jnp.float32)
    activated, backward = jax.vjp(jax.nn.gelu, pre)
    activated = activated.astype(jnp.bfloat16)
    out = jnp.dot(activated, ocean_w_out, preferred_element_type=jnp.float32)
    ocean_out = (
        ((flat_field.astype(jnp.float32) + out) * flat_wet)
        .astype(jnp.bfloat16)
        .reshape(tile_x, tile_y, channels)
    )
    dout = (ocean_cotangent.reshape(cells, channels).astype(jnp.float32) * flat_wet).astype(
        jnp.bfloat16
    )
    dact = lax.dot_general(
        dout, ocean_w_out, (((1,), (1,)), ((), ())), preferred_element_type=jnp.float32
    )
    dpre = backward(dact)[0].astype(jnp.bfloat16)
    grad_in = lax.dot_general(
        dpre, ocean_normed, (((0,), (0,)), ((), ())), preferred_element_type=jnp.float32
    )
    grad_out = lax.dot_general(
        activated, dout, (((0,), (0,)), ((), ())), preferred_element_type=jnp.float32
    )
    terms = jnp.concatenate([grad_in, grad_out], axis=0)
    weight_grads = lax.psum_scatter(terms, ("grp", "tile", "tp"), scatter_dimension=0, tiled=True)
    return (atmos_out, ocean_out, weight_grads)


def solution(mesh):
    in_specs = (
        P(("grp", "tile"), None),
        P(),
        P(("grp", "tile"), "tp"),
        P(("grp", "tile"), "tp"),
        P(),
        P(("grp", "tile", "tp"), None),
        P(("grp", "tile", "tp"), None, None, None),
        P(("grp", "tile"), "tp", None),
        P(("grp", "tile"), "tp"),
        P(),
        P(),
        P(),
        P(),
        P(("grp", "tile"), "tp", None),
    )
    out_specs = (
        P(("grp", "tile", "tp"), None),
        P(("grp", "tile"), "tp", None),
        P(("grp", "tile", "tp"), None),
    )
    return jax.shard_map(
        on_device, mesh=mesh, in_specs=in_specs, out_specs=out_specs, check_vma=False
    )
```

profile of v0, /device:TPU:0, one launch (start us, length us, event | category | flops | bytes accessed | tf_op | source)
XLA Modules:
  0.0 300.5 jit_solution(9202283299108384426)
XLA Ops:
  7.2 0.7 all-gather.5.cloned.1.call-update
  8.0 0.7 all-gather.3.cloned.1.call-update
  8.7 1.8 fusion
  10.5 31.0 %all-gather.5.cloned.1.call-done = bf16[1536,768]{1,0:T(8,128)(2,1)} async-done(((bf16[192,768]{1,0:T(8,128)(2,1)}), bf16[1536,768]{1,0:T(8,128)(2,1)}) %all-gather.5.cloned.1.call-update) | async-done | bytes 2359312 | tf_op jit(solution)/shard_map/all_gather | solution.py:55
  41.5 30.8 %all-gather.3.cloned.1.call-done = bf16[1536,768]{1,0:T(8,128)(2,1)} async-done(((bf16[192,768]{1,0:T(8,128)(2,1)}), bf16[1536,768]{1,0:T(8,128)(2,1)}) %all-gather.3.cloned.1.call-update) | async-done | bytes 2359312 | tf_op jit(solution)/shard_map/all_gather | solution.py:49
  72.3 6.9 %convolution_convert_fusion = bf16[512,1536]{1,0:T(8,128)(2,1)} fusion(bf16[1536,768]{1,0:T(8,128)(2,1)} %all-gather.5.cloned.1.call-done, bf16[1536,768]{1,0:T(8,128)(2,1)} %all-gather.3.cloned.1.call-done, bf16[512,1536]{1,0:T(8,128)(2,1)S(1)} %copy-done.1, f32[1536]{0:T(1024)S(1)} %copy-done.12, f32[512]{0:T(512)S(1)} %add_rsqrt_fusion.1), kind=kOutput, calls=%fused_computation.5 | convolution fusion | flops 2423390208 | bytes 7872512 | tf_op jit(solution)/shard_map/dot_general | solution.py:53
  79.3 0.6 copy-done.7
  80.0 34.8 %reduce-scatter.3.cloned.1.call-done = bf16[128,1536]{1,0:T(8,128)(2,1)} async-done(((bf16[512,1536]{1,0:T(8,128)(2,1)}), bf16[128,1536]{1,0:T(8,128)(2,1)}) %reduce-scatter.3.cloned.1.call-update) | async-done | bytes 393232 | tf_op jit(solution)/shard_map/reduce_scatter | solution.py:62
  114.8 1.1 add_convert_fusion
  116.0 0.3 convolution_convert_fusion.1
  116.3 14.6 %all_gather.11 = bf16[512,256]{1,0:T(8,128)(2,1)S(1)} all-gather(bf16[128,256]{1,0:T(8,128)(2,1)S(1)} %convolution_convert_fusion.1), channel_id=1, replica_groups=mesh['grp'=2,'tile'=4,'tp'=4] {'tp'}, dimensions={0}, use_global_device_ids=true | all-gather | bytes 327680 | tf_op jit(solution)/shard_map/all_gather | solution.py:68
  130.8 0.4 fusion.41
  131.2 0.2 fusion.19
  131.5 0.1 select_convert_fusion
  131.6 1.3 collective-permute-start.1
  132.9 3.0 %collective-permute-start = (bf16[1,32,256]{2,1,0:T(8,128)(2,1)S(1)}, bf16[1,32,256]{2,1,0:T(8,128)(2,1)S(1)}, u32[]{:S(2)}, u32[]{:S(2)}) collective-permute-start(bf16[1,32,256]{2,1,0:T(8,128)(2,1)S(1)} %get-tuple-element.7), channel_id=1, source_target_pairs={{0,4},{4,8},{8,12},{12,16},{16,20},{20,24},{24,28},{1,5},{5,9},{9,... | collective-permute-start | bytes 49160 | tf_op jit(solution)/shard_map/ppermute | solution.py:15
  136.1 0.7 collective-permute-done
  136.8 1.3 collective-permute-start.3
  138.1 4.5 %collective-permute-start.2 = (bf16[10,1,256]{2,1,0:T(2,128)(2,1)S(1)}, bf16[10,1,256]{2,1,0:T(2,128)(2,1)S(1)}, u32[]{:S(2)}, u32[]{:S(2)}) collective-permute-start(bf16[10,1,256]{2,1,0:T(2,128)(2,1)S(1)} %get-tuple-element.5), channel_id=1, source_target_pairs={{0,1},{1,2},{2,3},{4,5},{5,6},{6,7},{8,9},{9,10},{10,11},{12,13},{... | collective-permute-start | bytes 15368 | tf_op jit(solution)/shard_map/ppermute | solution.py:15
  142.7 1.3 collective-permute-done.2
  144.1 0.3 fusion.57
  144.4 0.2 multiply_reduce_fusion
  144.6 0.2 copy-done.10
  144.8 0.1 multiply_convert_fusion.1
  144.9 0.2 copy-done.3
  145.1 0.3 fusion.63
  145.4 0.6 fusion.56
  146.0 3.1 %fusion.30 = f32[1024,256]{1,0:T(8,128)} fusion(bf16[256,256]{1,0:T(8,128)(2,1)S(1)} %bitcast.50, f32[256,1024]{1,0:T(8,128)S(1)} %fusion.63, bf16[256,256]{1,0:T(8,128)(2,1)S(1)} %fusion.32, bf16[1024,256]{1,0:T(8,128)(2,1)} %param.26), kind=kOutput, calls=%fused_computation.38 | convolution fusion | flops 273678336 | bytes 2883584 | tf_op jit(solution)/shard_map/dot_general | solution.py:117
  149.2 2.7 pad_maximum_fusion
  151.9 1.0 copy-done.11
  152.9 1.1 fusion.20
  154.0 139.9 %reduce-scatter.5.cloned.1.call-done = f32[64,256]{1,0:T(8,128)} async-done(((f32[2048,256]{1,0:T(8,128)}), f32[64,256]{1,0:T(8,128)}) %reduce-scatter.5.cloned.1.call-update) | async-done | bytes 65552 | tf_op jit(solution)/shard_map/reduce_scatter | solution.py:124
  (40 shorter events, 0.6 us)
Async XLA Ops:
  7.2 108.8 %copy-start = (bf16[1536,256]{1,0:T(8,128)(2,1)S(1)}, bf16[1536,256]{1,0:T(8,128)(2,1)}, u32[]{:S(2)}) copy-start(bf16[1536,256]{1,0:T(8,128)(2,1)} %param.18) | copy-start | bytes 2359300
  7.2 65.1 %copy-start.1 = (bf16[512,1536]{1,0:T(8,128)(2,1)S(1)}, bf16[512,1536]{1,0:T(8,128)(2,1)}, u32[]{:S(2)}) copy-start(bf16[512,1536]{1,0:T(8,128)(2,1)} %param.14) | copy-start | bytes 4718596
  7.2 65.1 %copy-start.12 = (f32[1536]{0:T(1024)S(1)}, f32[1536]{0:T(1024)}, u32[]{:S(2)}) copy-start(f32[1536]{0:T(1024)} %param.15) | copy-start | bytes 18436
  7.2 34.3 %all-gather.5.cloned.1.call-start = ((), (), s32[]{:S(2)}) async-start(), calls=%async_computation.3 | async-start | bytes 2654208 | tf_op jit(solution)/shard_map/all_gather | solution.py:55
  7.9 64.4 %all-gather.3.cloned.1.call-start = ((), (), s32[]{:S(2)}) async-start(), calls=%async_computation.2 | async-start | bytes 2654208 | tf_op jit(solution)/shard_map/all_gather | solution.py:49
  8.7 106.1 %reduce-scatter.3.cloned.1.call-start = ((), (), s32[]{:S(2)}) async-start(), calls=%async_computation.4 | async-start | bytes 1966080 | tf_op jit(solution)/shard_map/reduce_scatter | solution.py:62
  79.2 0.7 copy-start.7
  79.2 51.6 %copy-start.9 = (s32[2,3]{1,0:T(2,128)S(1)}, s32[2,3]{1,0:T(2,128)}, u32[]{:S(2)}) copy-start(s32[2,3]{1,0:T(2,128)} %param.19) | copy-start | bytes 76
  79.2 214.7 %reduce-scatter.5.cloned.1.call-start = ((), (), s32[]{:S(2)}) async-start(), calls=%async_computation.5 | async-start | bytes 2162688 | tf_op jit(solution)/shard_map/reduce_scatter | solution.py:124
  80.0 51.2 %copy-start.4 = (bf16[2,3,128,128]{3,2,1,0:T(8,128)(2,1)S(1)}, bf16[2,3,128,128]{3,2,1,0:T(8,128)(2,1)}, u32[]{:S(2)}) copy-start(bf16[2,3,128,128]{3,2,1,0:T(8,128)(2,1)} %param.20) | copy-start | bytes 589828
  115.9 15.5 %copy-start.2 = (bf16[128,1536]{1,0:T(8,128)(2,1)}, bf16[128,1536]{1,0:T(8,128)(2,1)S(1)}, u32[]{:S(2)}) copy-start(bf16[128,1536]{1,0:T(8,128)(2,1)S(1)} %add_convert_fusion) | copy-start | bytes 1179652
  115.9 15.5 %copy-start.6 = (bf16[8,32,256]{2,1,0:T(8,128)(2,1)S(1)}, bf16[8,32,256]{2,1,0:T(8,128)(2,1)}, u32[]{:S(2)}) copy-start(bf16[8,32,256]{2,1,0:T(8,128)(2,1)} %param.21) | copy-start | bytes 393220
  116.2 19.7 %copy-start.5 = (bf16[8,32,256]{2,1,0:T(8,128)(2,1)S(1)}, bf16[8,32,256]{2,1,0:T(8,128)(2,1)}, u32[]{:S(2)}) copy-start(bf16[8,32,256]{2,1,0:T(8,128)(2,1)} %param.27) | copy-start | bytes 393220
  116.3 26.4 %copy-start.8 = (f32[3,3,256]{2,1,0:T(4,128)S(1)}, f32[3,3,256]{2,1,0:T(4,128)}, u32[]{:S(2)}) copy-start(f32[3,3,256]{2,1,0:T(4,128)} %param.23) | copy-start | bytes 27652
  131.6 4.5 %collective-permute-start.1 = (bf16[1,32,256]{2,1,0:T(8,128)(2,1)S(1)}, bf16[1,32,256]{2,1,0:T(8,128)(2,1)S(1)}, u32[]{:S(2)}, u32[]{:S(2)}) collective-permute-start(bf16[1,32,256]{2,1,0:T(8,128)(2,1)S(1)} %get-tuple-element.8), channel_id=1, source_target_pairs={{4,0},{8,4},{12,8},{16,12},{20,16},{24,20},{28,24},{5,1},{9,5},{13... | collective-permute-start | bytes 49160 | tf_op jit(solution)/shard_map/ppermute | solution.py:18
  132.9 3.9 %collective-permute-start = (bf16[1,32,256]{2,1,0:T(8,128)(2,1)S(1)}, bf16[1,32,256]{2,1,0:T(8,128)(2,1)S(1)}, u32[]{:S(2)}, u32[]{:S(2)}) collective-permute-start(bf16[1,32,256]{2,1,0:T(8,128)(2,1)S(1)} %get-tuple-element.7), channel_id=1, source_target_pairs={{0,4},{4,8},{8,12},{12,16},{16,20},{20,24},{24,28},{1,5},{5,9},{9,... | collective-permute-start | bytes 49160 | tf_op jit(solution)/shard_map/ppermute | solution.py:15
  136.8 5.9 %collective-permute-start.3 = (bf16[10,1,256]{2,1,0:T(2,128)(2,1)S(1)}, bf16[10,1,256]{2,1,0:T(2,128)(2,1)S(1)}, u32[]{:S(2)}, u32[]{:S(2)}) collective-permute-start(bf16[10,1,256]{2,1,0:T(2,128)(2,1)S(1)} %get-tuple-element.6), channel_id=1, source_target_pairs={{1,0},{2,1},{3,2},{5,4},{6,5},{7,6},{9,8},{10,9},{11,10},{13,12},{... | collective-permute-start | bytes 15368 | tf_op jit(solution)/shard_map/ppermute | solution.py:18
  138.1 5.9 %collective-permute-start.2 = (bf16[10,1,256]{2,1,0:T(2,128)(2,1)S(1)}, bf16[10,1,256]{2,1,0:T(2,128)(2,1)S(1)}, u32[]{:S(2)}, u32[]{:S(2)}) collective-permute-start(bf16[10,1,256]{2,1,0:T(2,128)(2,1)S(1)} %get-tuple-element.5), channel_id=1, source_target_pairs={{0,1},{1,2},{2,3},{4,5},{5,6},{6,7},{8,9},{9,10},{10,11},{12,13},{... | collective-permute-start | bytes 15368 | tf_op jit(solution)/shard_map/ppermute | solution.py:15
  144.1 0.7 copy-start.10
  144.1 1.0 copy-start.3
  151.9 1.0 copy-start.11
Sparse Core Ops, SparseCore 0:
  9.9 31.5 all-gather.4
  43.4 28.8 all-gather.2
  79.3 35.4 reduce-scatter.2
  152.0 141.8 reduce-scatter.4
where the time goes:
time: 301 us; the launch traced here: 300 us
  waiting for transfers between devices  240 us (80%)
  blocking collectives  14.6 us (5%)
  between operations  14 us (5%)
  matrix products  12.9 us (4%)
  starting transfers between devices  10.3 us (3%)
  other arithmetic  6.51 us (2%)
    reduce_scatter x1, waiting for transfers between devices, on_device(): lax.psum_scatter(terms, ('grp', 'tile', 'tp'), scatter_dimension=0, tiled...  140 us
    reduce_scatter x1, waiting for transfers between devices, on_device(): lax.psum_scatter(partial_sum.astype(jnp.bfloat16), 'tp', scatter_dimensio...  34.8 us
    all_gather x1, waiting for transfers between devices, on_device(): lax.all_gather(w_second, ('grp', 'tile'), axis=0, tiled=True)  31 us
    all_gather x1, waiting for transfers between devices, on_device(): lax.all_gather(w_first, ('grp', 'tile'), axis=0, tiled=True)  30.8 us
    all_gather x1, blocking collectives, on_device(): piece = lax.all_gather(flux, 'tp', axis=0, tiled=True)  14.6 us
    ppermute x2, starting transfers between devices, with_halo(): lax.ppermute(lax.slice_in_dim(block, block.shape[dim] - width, None, axis...  7.58 us
    dot_general x1, matrix products, on_device(): lax.dot_general(hidden, lax.all_gather(w_second, ('grp', 'tile'), axis=0,...  6.86 us
  transfers between devices with their start and end apart: 8, of which 6 were waited for; matrix products, arithmetic and copies ran while one was open for 1% of the time, Pallas kernels for 0%

commit v1 on v0

--- a/solution.py
+++ b/solution.py
@@ -5,6 +5,18 @@
 
 LEV = 16
 epsilon = 1e-06
+
+
+def gather_by_bits(value, axis, dim):
+    ways, here, step = (lax.axis_size(axis), lax.axis_index(axis), value.shape[dim])
+    line, have = (value, 1)
+    while have < ways:
+        line = jnp.concatenate(
+            [line, lax.ppermute(line, axis, [(d, (d - have) % ways) for d in range(ways)])],
+            axis=dim,
+        )
+        have = 2 * have
+    return jnp.roll(line, here * step, axis=dim)
 
 
 def with_halo(block, sides, width):
@@ -52,7 +64,7 @@
     hidden = jax.nn.gelu(hsum).astype(jnp.bfloat16)
     partial_sum = lax.dot_general(
         hidden,
-        lax.all_gather(w_second, ("grp", "tile"), axis=0, tiled=True),
+        gather_by_bits(w_second, ("grp", "tile"), 0),
         (((1,), (1,)), ((), ())),
         preferred_element_type=jnp.float32,
     )

time: 301 us -> 305 us (1.013)
  waiting for transfers between devices: 240 us -> 230 us
  local copies, waits for them, and re-layouts: 2.17 us -> 7 us
  starting transfers between devices: 10.3 us -> 15.1 us
  other arithmetic: 6.51 us -> 9.71 us
    ppermute x0 -> x3, waiting for transfers between devices: none -> 52 us  [gather_by_bits(): lax.ppermute(line, axis, [(d, (d - have) % ways) for d in range(ways)])]
    all_gather x1 -> x0, waiting for transfers between devices: 31 us -> none  [on_device(): lax.all_gather(w_second, ('grp', 'tile'), axis=0, tiled=True)]
    all_gather x1, waiting for transfers between devices: 30.8 us -> 0.01 us  [on_device(): lax.all_gather(w_first, ('grp', 'tile'), axis=0, tiled=True)]
    ppermute x0 -> x3, starting transfers between devices: none -> 4.67 us  [gather_by_bits(): lax.ppermute(line, axis, [(d, (d - have) % ways) for d in range(ways)])]
    unnamed x26 -> x31, local copies, waits for them, and re-layouts: 2.08 us -> 5.81 us
    concatenate x0 -> x2, other arithmetic: none -> 3.09 us  [gather_by_bits(): jnp.concatenate([line, lax.ppermute(line, axis, [(d, (d - have) % ways) f...]
  transfers between devices with their start and end apart: 8 -> 10, of which waited for: 6 -> 7; matrix products, arithmetic and copies ran while one was open for 1% -> 5% of each run, Pallas kernels for 0% -> 0%
where the time goes in v1:
time: 305 us
  waiting for transfers between devices  230 us (75%)
  starting transfers between devices  15.1 us (5%)
  matrix products  14.5 us (5%)
  blocking collectives  14.4 us (5%)
  between operations  14 us (5%)
  other arithmetic  9.71 us (3%)
  local copies, waits for them, and re-layouts  7 us (2%)
    reduce_scatter x1, waiting for transfers between devices, on_device(): lax.psum_scatter(terms, ('grp', 'tile', 'tp'), scatter_dimension=0, tiled...  140 us
    ppermute x3, waiting for transfers between devices, gather_by_bits(): lax.ppermute(line, axis, [(d, (d - have) % ways) for d in range(ways)])  52 us
    reduce_scatter x1, waiting for transfers between devices, on_device(): lax.psum_scatter(partial_sum.astype(jnp.bfloat16), 'tp', scatter_dimensio...  35.7 us
    all_gather x1, blocking collectives, on_device(): piece = lax.all_gather(flux, 'tp', axis=0, tiled=True)  14.4 us
    ppermute x2, starting transfers between devices, with_halo(): lax.ppermute(lax.slice_in_dim(block, block.shape[dim] - width, None, axis...  7.58 us
    dot_general x1, matrix products, on_device(): lax.dot_general(hidden, gather_by_bits(w_second, ('grp', 'tile'), 0), (((...  7.46 us
  transfers between devices with their start and end apart: 10, of which 7 were waited for; matrix products, arithmetic and copies ran while one was open for 5% of the time, Pallas kernels for 0%

profile of v1, /device:TPU:0, one launch (start us, length us, event | category | flops | bytes accessed | tf_op | source)
XLA Modules:
  0.0 304.9 jit_solution(11417044663771471322)
XLA Ops:
  7.2 0.7 all-gather.2.cloned.1.call-update
  8.0 3.4 %collective-permute-start = (bf16[192,768]{1,0:T(8,128)(2,1)}, bf16[192,768]{1,0:T(8,128)(2,1)S(1)}, u32[]{:S(2)}, u32[]{:S(2)}) collective-permute-start(bf16[192,768]{1,0:T(8,128)(2,1)} %param.17), channel_id=1, source_target_pairs={{0,28},{4,0},{8,4},{12,8},{16,12},{20,16},{24,20},{28,24},{1,29},{... | collective-permute-start | bytes 884744 | tf_op jit(solution)/shard_map/ppermute | solution.py:15
  11.4 4.6 %collective-permute-done = bf16[192,768]{1,0:T(8,128)(2,1)S(1)} collective-permute-done((bf16[192,768]{1,0:T(8,128)(2,1)}, bf16[192,768]{1,0:T(8,128)(2,1)S(1)}, u32[]{:S(2)}, u32[]{:S(2)}) %collective-permute-start) | collective-permute-done | bytes 294944 | tf_op jit(solution)/shard_map/ppermute | solution.py:15
  15.9 1.0 pad_maximum_fusion.2
  16.9 0.6 collective-permute-start.1
  17.6 18.2 %collective-permute-done.1 = bf16[384,768]{1,0:T(8,128)(2,1)S(1)} collective-permute-done((bf16[384,768]{1,0:T(8,128)(2,1)S(1)}, bf16[384,768]{1,0:T(8,128)(2,1)S(1)}, u32[]{:S(2)}, u32[]{:S(2)}) %collective-permute-start.1) | collective-permute-done | bytes 589856 | tf_op jit(solution)/shard_map/ppermute | solution.py:15
  35.8 2.1 pad_maximum_fusion.1
  37.9 0.6 collective-permute-start.2
  38.5 0.7 constant_dynamic-update-slice_fusion.7
  39.2 1.8 fusion
  41.0 0.7 constant_dynamic-update-slice_fusion.6
  41.8 0.9 constant_dynamic-update-slice_fusion.5
  42.6 29.2 %collective-permute-done.2 = bf16[768,768]{1,0:T(8,128)(2,1)S(1)} collective-permute-done((bf16[768,768]{1,0:T(8,128)(2,1)}, bf16[768,768]{1,0:T(8,128)(2,1)S(1)}, u32[]{:S(2)}, u32[]{:S(2)}) %collective-permute-start.2) | collective-permute-done | bytes 1179680 | tf_op jit(solution)/shard_map/ppermute | solution.py:15
  71.8 1.1 constant_dynamic-update-slice_fusion.4
  72.9 0.7 constant_dynamic-update-slice_fusion.3
  73.7 0.7 constant_dynamic-update-slice_fusion.2
  74.4 0.9 constant_dynamic-update-slice_fusion.1
  75.3 1.1 constant_dynamic-update-slice_fusion
  76.4 7.5 %convolution_convert_fusion = bf16[512,1536]{1,0:T(8,128)(2,1)} fusion(bf16[3072,768]{1,0:T(8,128)(2,1)} %constant_dynamic-update-slice_fusion, s32[]{:T(128)S(6)} %select_n.29, bf16[1536,768]{1,0:T(8,128)(2,1)} %all-gather.2.cloned.1.call-done, bf16[512,1536]{1,0:T(8,128)(2,1)} %param.14, f32[1536]{0:T(1024)S(1)} %copy-done.11, f32[512]{0:T(512)S(1)} %add_rsqrt_fusion.1), kind=kOutput, calls=%fused_computation.5 | convolution fusion | flops 2423390208 | bytes 7872516 | tf_op jit(solution)/shard_map/dot_general | solution.py:65
  84.0 35.7 %reduce-scatter.3.cloned.1.call-done = bf16[128,1536]{1,0:T(8,128)(2,1)} async-done(((bf16[512,1536]{1,0:T(8,128)(2,1)}), bf16[128,1536]{1,0:T(8,128)(2,1)}) %reduce-scatter.3.cloned.1.call-update) | async-done | bytes 393232 | tf_op jit(solution)/shard_map/reduce_scatter | solution.py:74
  119.7 1.2 add_convert_fusion
  121.2 14.4 %all_gather.7 = bf16[512,256]{1,0:T(8,128)(2,1)S(1)} all-gather(bf16[128,256]{1,0:T(8,128)(2,1)S(1)} %convolution_convert_fusion.1), channel_id=1, replica_groups=mesh['grp'=2,'tile'=4,'tp'=4] {'tp'}, dimensions={0}, use_global_device_ids=true | all-gather | bytes 327680 | tf_op jit(solution)/shard_map/all_gather | solution.py:80
  136.4 1.4 collective-permute-start.4
  137.9 3.0 collective-permute-start.3
  141.0 0.7 collective-permute-done.3
  141.7 1.3 collective-permute-start.6
  143.0 4.5 %collective-permute-start.5 = (bf16[10,1,256]{2,1,0:T(2,128)(2,1)S(1)}, bf16[10,1,256]{2,1,0:T(2,128)(2,1)S(1)}, u32[]{:S(2)}, u32[]{:S(2)}) collective-permute-start(bf16[10,1,256]{2,1,0:T(2,128)(2,1)S(1)} %get-tuple-element.5), channel_id=1, source_target_pairs={{0,1},{1,2},{2,3},{4,5},{5,6},{6,7},{8,9},{9,10},{10,11},{12,13},{... | collective-permute-start | bytes 15368 | tf_op jit(solution)/shard_map/ppermute | solution.py:27
  147.6 1.3 collective-permute-done.5
  150.6 3.1 %fusion.31 = f32[1024,256]{1,0:T(8,128)} fusion(bf16[256,256]{1,0:T(8,128)(2,1)S(1)} %bitcast.49, f32[256,1024]{1,0:T(8,128)S(1)} %fusion.65, bf16[256,256]{1,0:T(8,128)(2,1)S(1)} %fusion.33, bf16[1024,256]{1,0:T(8,128)(2,1)} %param.26), kind=kOutput, calls=%fused_computation.41 | convolution fusion | flops 273678336 | bytes 2883584 | tf_op jit(solution)/shard_map/dot_general | solution.py:129
  153.7 2.7 pad_maximum_fusion
  156.4 2.2 fusion.21
  158.6 139.8 %reduce-scatter.5.cloned.1.call-done = f32[64,256]{1,0:T(8,128)} async-done(((f32[2048,256]{1,0:T(8,128)}), f32[64,256]{1,0:T(8,128)}) %reduce-scatter.5.cloned.1.call-update) | async-done | bytes 65552 | tf_op jit(solution)/shard_map/reduce_scatter | solution.py:136
  (51 shorter events, 3.0 us)
Async XLA Ops:
  7.2 113.7 %copy-start = (bf16[1536,256]{1,0:T(8,128)(2,1)S(1)}, bf16[1536,256]{1,0:T(8,128)(2,1)}, u32[]{:S(2)}) copy-start(bf16[1536,256]{1,0:T(8,128)(2,1)} %param.18) | copy-start | bytes 2359300
  7.2 31.3 %copy-start.1 = (bf16[192,768]{1,0:T(8,128)(2,1)S(1)}, bf16[192,768]{1,0:T(8,128)(2,1)}, u32[]{:S(2)}) copy-start(bf16[192,768]{1,0:T(8,128)(2,1)} %param.17) | copy-start | bytes 884740
  7.2 69.2 %all-gather.2.cloned.1.call-start = ((), (), s32[]{:S(2)}) async-start(), calls=%async_computation.2 | async-start | bytes 2654208 | tf_op jit(solution)/shard_map/all_gather | solution.py:61
  7.9 111.8 %reduce-scatter.3.cloned.1.call-start = ((), (), s32[]{:S(2)}) async-start(), calls=%async_computation.3 | async-start | bytes 1966080 | tf_op jit(solution)/shard_map/reduce_scatter | solution.py:74
  8.0 8.0 %collective-permute-start = (bf16[192,768]{1,0:T(8,128)(2,1)}, bf16[192,768]{1,0:T(8,128)(2,1)S(1)}, u32[]{:S(2)}, u32[]{:S(2)}) collective-permute-start(bf16[192,768]{1,0:T(8,128)(2,1)} %param.17), channel_id=1, source_target_pairs={{0,28},{4,0},{8,4},{12,8},{16,12},{20,16},{24,20},{28,24},{1,29},{... | collective-permute-start | bytes 884744 | tf_op jit(solution)/shard_map/ppermute | solution.py:15
  16.9 18.8 %collective-permute-start.1 = (bf16[384,768]{1,0:T(8,128)(2,1)S(1)}, bf16[384,768]{1,0:T(8,128)(2,1)S(1)}, u32[]{:S(2)}, u32[]{:S(2)}) collective-permute-start(bf16[384,768]{1,0:T(8,128)(2,1)S(1)} %pad_maximum_fusion.2), channel_id=1, source_target_pairs={{0,24},{4,28},{8,0},{12,4},{16,8},{20,12},{24,16},{28,20},{1,25},{... | collective-permute-start | bytes 1769480 | tf_op jit(solution)/shard_map/ppermute | solution.py:15
  37.9 33.9 %collective-permute-start.2 = (bf16[768,768]{1,0:T(8,128)(2,1)}, bf16[768,768]{1,0:T(8,128)(2,1)S(1)}, u32[]{:S(2)}, u32[]{:S(2)}) collective-permute-start(bf16[768,768]{1,0:T(8,128)(2,1)} %pad_maximum_fusion.1), channel_id=1, source_target_pairs={{0,16},{4,20},{8,24},{12,28},{16,0},{20,4},{24,8},{28,12},{1,17},{... | collective-permute-start | bytes 3538952 | tf_op jit(solution)/shard_map/ppermute | solution.py:15
  72.9 3.4 %copy-start.11 = (f32[1536]{0:T(1024)S(1)}, f32[1536]{0:T(1024)}, u32[]{:S(2)}) copy-start(f32[1536]{0:T(1024)} %param.15) | copy-start | bytes 18436
  76.4 7.6 %copy-start.7 = (s32[8,32]{1,0:T(8,128)S(1)}, s32[8,32]{1,0:T(8,128)}, u32[]{:S(2)}) copy-start(s32[8,32]{1,0:T(8,128)} %param.22) | copy-start | bytes 3076
  83.8 51.8 %copy-start.9 = (s32[2,3]{1,0:T(2,128)S(1)}, s32[2,3]{1,0:T(2,128)}, u32[]{:S(2)}) copy-start(s32[2,3]{1,0:T(2,128)} %param.19) | copy-start | bytes 76
  83.8 52.2 %copy-start.4 = (bf16[2,3,128,128]{3,2,1,0:T(8,128)(2,1)S(1)}, bf16[2,3,128,128]{3,2,1,0:T(8,128)(2,1)}, u32[]{:S(2)}) copy-start(bf16[2,3,128,128]{3,2,1,0:T(8,128)(2,1)} %param.20) | copy-start | bytes 589828
  83.9 52.4 %copy-start.6 = (bf16[8,32,256]{2,1,0:T(8,128)(2,1)S(1)}, bf16[8,32,256]{2,1,0:T(8,128)(2,1)}, u32[]{:S(2)}) copy-start(bf16[8,32,256]{2,1,0:T(8,128)(2,1)} %param.21) | copy-start | bytes 393220
  83.9 214.5 %reduce-scatter.5.cloned.1.call-start = ((), (), s32[]{:S(2)}) async-start(), calls=%async_computation.4 | async-start | bytes 2162688 | tf_op jit(solution)/shard_map/reduce_scatter | solution.py:136
  84.0 56.9 %copy-start.5 = (bf16[8,32,256]{2,1,0:T(8,128)(2,1)S(1)}, bf16[8,32,256]{2,1,0:T(8,128)(2,1)}, u32[]{:S(2)}) copy-start(bf16[8,32,256]{2,1,0:T(8,128)(2,1)} %param.27) | copy-start | bytes 393220
  120.9 28.1 %copy-start.2 = (bf16[128,1536]{1,0:T(8,128)(2,1)}, bf16[128,1536]{1,0:T(8,128)(2,1)S(1)}, u32[]{:S(2)}) copy-start(bf16[128,1536]{1,0:T(8,128)(2,1)S(1)} %add_convert_fusion) | copy-start | bytes 1179652
  120.9 26.7 %copy-start.8 = (f32[3,3,256]{2,1,0:T(4,128)S(1)}, f32[3,3,256]{2,1,0:T(4,128)}, u32[]{:S(2)}) copy-start(f32[3,3,256]{2,1,0:T(4,128)} %param.23) | copy-start | bytes 27652
  136.3 13.3 %copy-start.10 = (f32[256]{0:T(256)S(1)}, f32[256]{0:T(256)}, u32[]{:S(2)}) copy-start(f32[256]{0:T(256)} %param.24) | copy-start | bytes 3076
  136.4 13.3 %copy-start.3 = (bf16[256,1024]{1,0:T(8,128)(2,1)S(1)}, bf16[256,1024]{1,0:T(8,128)(2,1)}, u32[]{:S(2)}) copy-start(bf16[256,1024]{1,0:T(8,128)(2,1)} %param.25) | copy-start | bytes 1572868
  136.4 4.6 %collective-permute-start.4 = (bf16[1,32,256]{2,1,0:T(8,128)(2,1)S(1)}, bf16[1,32,256]{2,1,0:T(8,128)(2,1)S(1)}, u32[]{:S(2)}, u32[]{:S(2)}) collective-permute-start(bf16[1,32,256]{2,1,0:T(8,128)(2,1)S(1)} %get-tuple-element.8), channel_id=1, source_target_pairs={{4,0},{8,4},{12,8},{16,12},{20,16},{24,20},{28,24},{5,1},{9,5},{13... | collective-permute-start | bytes 49160 | tf_op jit(solution)/shard_map/ppermute | solution.py:30
  137.9 3.9 %collective-permute-start.3 = (bf16[1,32,256]{2,1,0:T(8,128)(2,1)S(1)}, bf16[1,32,256]{2,1,0:T(8,128)(2,1)S(1)}, u32[]{:S(2)}, u32[]{:S(2)}) collective-permute-start(bf16[1,32,256]{2,1,0:T(8,128)(2,1)S(1)} %get-tuple-element.7), channel_id=1, source_target_pairs={{0,4},{4,8},{8,12},{12,16},{16,20},{20,24},{24,28},{1,5},{5,9},{9,... | collective-permute-start | bytes 49160 | tf_op jit(solution)/shard_map/ppermute | solution.py:27
  141.7 5.9 %collective-permute-start.6 = (bf16[10,1,256]{2,1,0:T(2,128)(2,1)S(1)}, bf16[10,1,256]{2,1,0:T(2,128)(2,1)S(1)}, u32[]{:S(2)}, u32[]{:S(2)}) collective-permute-start(bf16[10,1,256]{2,1,0:T(2,128)(2,1)S(1)} %get-tuple-element.6), channel_id=1, source_target_pairs={{1,0},{2,1},{3,2},{5,4},{6,5},{7,6},{9,8},{10,9},{11,10},{13,12},{... | collective-permute-start | bytes 15368 | tf_op jit(solution)/shard_map/ppermute | solution.py:30
  143.0 5.9 %collective-permute-start.5 = (bf16[10,1,256]{2,1,0:T(2,128)(2,1)S(1)}, bf16[10,1,256]{2,1,0:T(2,128)(2,1)S(1)}, u32[]{:S(2)}, u32[]{:S(2)}) collective-permute-start(bf16[10,1,256]{2,1,0:T(2,128)(2,1)S(1)} %get-tuple-element.5), channel_id=1, source_target_pairs={{0,1},{1,2},{2,3},{4,5},{5,6},{6,7},{8,9},{9,10},{10,11},{12,13},{... | collective-permute-start | bytes 15368 | tf_op jit(solution)/shard_map/ppermute | solution.py:27
Sparse Core Ops, SparseCore 0:
  9.9 48.6 all-gather.1
  84.0 35.6 reduce-scatter.2
  156.6 141.7 reduce-scatter.4
